TPU v7x, 512 devices: a whole 4x4x16 slice. The times are simulated.
512 devices in a mesh: vox: 512 (over y, z, x, core).
Axes of the slice: x: 4, y: 4, z: 16, core: 2. Of those that a mesh axis runs over, the one named last changes fastest.
Arguments:
- deform: bfloat16 [1048576, 1024], P('vox'), may hold values from -8 to 8
- sketch: bfloat16 [1024, 256], replicated, may hold values from -0.1875 to 0.1875
Outputs:
- factor_r: float32 [256, 256], replicated
- projected: float32 [1024, 256], P('vox')
All inputs are finite; a program needn't handle non-finite values.
Results may differ from a plain program's by a relative error of at most 0.0012.
Values sent between devices are 32-bit elements; how exact they have to be, the bound alone decides.
No kernel may reach another device: no remote copies, remote signals or barrier semaphores. Data moves between devices by JAX's collectives and lax.ppermute only.
A program may use at most 64 MiB of HBM per device.

v0:
```python
import jax
import jax.numpy as jnp
from jax import lax
from jax.sharding import Mesh
from jax.sharding import PartitionSpec as P

VOX = ("vox_0", "vox_1", "vox_2", "vox_3")


def in_blocks(shard, dim, length):
    before, after = (shard.shape[:dim], shard.shape[dim + 1 :])
    return jnp.moveaxis(shard.reshape(*before, length, -1, *after), dim, 0)


def sent_and_summed(shard, axis, dim):
    pieces = in_blocks(shard, dim, lax.axis_size(axis))
    arrived = lax.all_to_all(pieces, axis, split_axis=0, concat_axis=0, tiled=True)
    return arrived.sum(axis=0)


def sum_by_axis(shard, axes, dim):
    far, near = axes
    pieces = in_blocks(shard, dim, lax.axis_size(far))
    nearer = sent_and_summed(pieces, near, dim + 1)
    arrived = lax.all_to_all(nearer, far, split_axis=0, concat_axis=0, tiled=True)
    return arrived.sum(axis=0)


def rows_for(lines, length):
    spare = -lines.shape[0] % length
    if not spare:
        return lines
    return jnp.concatenate([lines, jnp.zeros((spare, *lines.shape[1:]), lines.dtype)])


def from_everyone(shard, axis):
    copies = jnp.broadcast_to(shard, (lax.axis_size(axis), *shard.shape))
    return lax.all_to_all(copies, axis, split_axis=0, concat_axis=0, tiled=True)


def in_order(pieces, dim):
    pieces = jnp.moveaxis(pieces, 0, dim)
    shape = pieces.shape
    return pieces.reshape(*shape[:dim], shape[dim] * shape[dim + 1], *shape[dim + 2 :])


def gather_axes(shard, axes, dim):
    far, near = axes
    leading = from_everyone(shard, far)
    pieces = jnp.swapaxes(from_everyone(leading, near), 0, 1)
    return in_order(pieces.reshape(-1, *shard.shape), dim)


def nested_sum(shard, axes):
    lines = shard.reshape(-1)
    padded = rows_for(lines, lax.axis_size(axes[0]) * lax.axis_size(axes[1]))
    whole = gather_axes(sum_by_axis(padded, axes, 0), axes, 0)
    return lax.slice_in_dim(whole, 0, len(lines)).reshape(shard.shape)


def inner_gram(left, right):
    return lax.dot_general(
        left,
        right,
        (((0,), (0,)), ((), ())),
        precision=lax.Precision.HIGHEST,
        preferred_element_type=jnp.float32,
    )


def split_pair(values):
    high = values.astype(jnp.bfloat16)
    rest = (values - high.astype(jnp.float32)).astype(jnp.bfloat16)
    return (high, rest)


def body(deform, sketch):
    devices = lax.axis_size(VOX)
    dims = (((0,), (0,)), ((), ()))
    sketched = jnp.dot(deform, sketch, preferred_element_type=jnp.float32)
    local_gram = inner_gram(sketched, sketched)
    sketch_high, sketch_rest = split_pair(sketched)
    cross = sum_by_axis(
        lax.dot_general(deform, sketch_high, dims, preferred_element_type=jnp.float32)
        + lax.dot_general(deform, sketch_rest, dims, preferred_element_type=jnp.float32),
        (("vox_0", "vox_1"), ("vox_2", "vox_3")),
        0,
    )
    total_gram = nested_sum(local_gram, (("vox_0", "vox_1"), ("vox_2", "vox_3")))
    lower = jnp.linalg.cholesky(total_gram)
    total_rows = sketched.shape[0] * devices
    factor_r = lower.T * (1.0 / jnp.sqrt(jnp.float32(total_rows)))
    projected = lax.linalg.triangular_solve(
        lower, cross, left_side=False, lower=True, transpose_a=True
    )
    return (factor_r, projected)


def solution(mesh):
    split = Mesh(mesh.devices.reshape(4, 16, 4, 2), ("vox_0", "vox_1", "vox_2", "vox_3"))
    in_specs = (P(VOX, None), P())
    out_specs = (P(), P(VOX, None))
    return jax.shard_map(body, mesh=split, in_specs=in_specs, out_specs=out_specs, check_vma=False)
```

profile of v0, /device:TPU:1, one launch (start us, length us, event | category | flops | bytes accessed | tf_op | source)
XLA Modules:
  0.0 159.7 jit_solution(983525974060181630)
XLA Ops:
  0.6 1.0 copy-done
  1.7 3.4 %fusion.14 = f32[2048,256]{1,0:T(8,128)S(1)} fusion(bf16[2048,1024]{1,0:T(8,128)(2,1)} %param.2, bf16[1024,256]{1,0:T(8,128)(2,1)S(1)} %copy-done), kind=kOutput, calls=%fused_computation.38 | convolution fusion | flops 1073741824 | bytes 6815744 | tf_op jit(solution)/shard_map/dot_general | solution.py:80
  5.1 3.5 %fusion.15 = f32[256,256]{1,0:T(8,128)S(1)} fusion(f32[2048,256]{1,0:T(8,128)S(1)} %fusion.14), kind=kOutput, calls=%fused_computation.39 | convolution fusion | flops 1610612736 | bytes 2359296 | tf_op jit(solution)/shard_map/dot_general | solution.py:62
  8.7 15.7 %all_to_all.38 = f32[8,64,128]{2,1,0:T(8,128)S(1)} all-to-all(f32[8,64,128]{2,1,0:T(8,128)S(1)} %bitcast.50), channel_id=1, replica_groups=mesh['vox_0'=4,'vox_1'=16,'vox_2'=4,'vox_3'=2] {'vox_2','vox_3'}, dimensions={0} | all-to-all | bytes 524288 | tf_op jit(solution)/shard_map/all_to_all | solution.py:17
  24.4 27.9 %all_to_all.39 = f32[64,1,128]{2,1,0:T(1,128)S(1)} all-to-all(f32[64,1,128]{2,1,0:T(1,128)S(1)} %bitcast.52), channel_id=1, replica_groups=mesh['vox_0'=4,'vox_1'=16,'vox_2'=4,'vox_3'=2] {'vox_0','vox_1'}, dimensions={0} | all-to-all | bytes 65536 | tf_op jit(solution)/shard_map/all_to_all | solution.py:25
  52.4 0.6 broadcast_in_dim.8
  53.1 4.6 %all-to-all-start.2 = ((f32[64,1,128]{2,1,0:T(1,128)}), f32[64,1,128]{2,1,0:T(1,128)S(1)}, u32[]{:S(2)}, u32[]{:S(2)}) async-start(f32[64,1,128]{2,1,0:T(1,128)} %broadcast_in_dim.8), calls=%async_computation.2 | async-start | bytes 65536 | tf_op jit(solution)/shard_map/all_to_all | solution.py:38
  57.7 4.5 %fusion.2 = f32[256,1024]{1,0:T(8,128)} fusion(bf16[2048,1024]{1,0:T(8,128)(2,1)} %param.2, f32[2048,256]{1,0:T(8,128)S(1)} %fusion.14), kind=kOutput, calls=%fused_computation.8 | convolution fusion | flops 1074266112 | bytes 7340032 | tf_op jit(solution)/shard_map/dot_general | solution.py:84
  62.1 8.8 %all-to-all-done.2 = f32[64,1,128]{2,1,0:T(1,128)S(1)} async-done(((f32[64,1,128]{2,1,0:T(1,128)}), f32[64,1,128]{2,1,0:T(1,128)S(1)}, u32[]{:S(2)}, u32[]{:S(2)}) %all-to-all-start.2) | async-done | bytes 32800 | tf_op jit(solution)/shard_map/all_to_all | solution.py:38
  70.9 0.7 broadcast_in_dim.9
  71.6 6.9 %all-to-all-start.3 = ((f32[8,64,128]{2,1,0:T(8,128)}), f32[8,64,128]{2,1,0:T(8,128)S(1)}, u32[]{:S(2)}, u32[]{:S(2)}) async-start(f32[8,64,128]{2,1,0:T(8,128)} %broadcast_in_dim.9), calls=%async_computation.3 | async-start | bytes 524288 | tf_op jit(solution)/shard_map/all_to_all | solution.py:38
  78.6 4.8 %fusion = f32[1024,256]{0,1:T(8,128)} fusion(f32[256,1024]{1,0:T(8,128)} %fusion.2, bf16[2048,1024]{1,0:T(8,128)(2,1)} %param.2, f32[2048,256]{1,0:T(8,128)S(1)} %fusion.14), kind=kOutput, calls=%fused_computation.4 | convolution fusion | flops 1076101120 | bytes 8388608 | tf_op jit(solution)/shard_map/dot_general | solution.py:85
  83.3 1.6 copy.24
  84.9 0.6 reshape_reshape.3
  85.5 1.4 copy.25
  86.9 4.8 %all-to-all-start.4 = ((f32[8,64,2,256]{3,2,1,0:T(2,128)}), f32[8,64,2,256]{3,2,1,0:T(2,128)S(1)}, u32[]{:S(2)}, u32[]{:S(2)}) async-start(f32[8,64,2,256]{3,2,1,0:T(2,128)} %copy.25), calls=%async_computation.4 | async-start | bytes 2097152 | tf_op jit(solution)/shard_map/all_to_all | solution.py:17
  92.2 11.7 %cholesky.50 = f32[128,128]{1,0:T(8,128)S(1)} custom-call(f32[128,128]{1,0:T(8,128)S(1)} %cholesky.118), custom_call_target="Cholesky" | custom-call | tf_op jit(solution)/shard_map/jit(cholesky)/cholesky | solution.py:90
  103.9 9.8 %custom-call.14 = f32[1,128,128]{1,2,0:T(8,128)S(1)} custom-call(f32[1,128,128]{2,1,0:T(8,128)S(1)} %get-tuple-element.35), custom_call_target="InvertDiagBlocksLowerTriangular" | custom-call | tf_op jit(solution)/shard_map/jit(cholesky)/cholesky | solution.py:90
  113.7 0.2 constant_dynamic-update-slice_fusion.1
  114.0 0.3 convolution_subtract_fusion
  114.2 11.7 %cholesky.105 = f32[128,128]{1,0:T(8,128)S(1)} custom-call(f32[128,128]{1,0:T(8,128)S(1)} %convolution_subtract_fusion), custom_call_target="Cholesky" | custom-call | tf_op jit(solution)/shard_map/jit(cholesky)/cholesky | solution.py:90
  126.0 0.6 compare_reduce_fusion
  128.0 0.8 copy.27
  128.8 1.1 reduce_sum.38
  129.9 4.9 %all-to-all-start.5 = ((f32[64,2,256]{2,1,0:T(2,128)}), f32[64,2,256]{2,1,0:T(2,128)S(1)}, u32[]{:S(2)}, u32[]{:S(2)}) async-start(f32[64,2,256]{2,1,0:T(2,128)} %reduce_sum.38), calls=%async_computation.5 | async-start | bytes 262144 | tf_op jit(solution)/shard_map/all_to_all | solution.py:25
  134.9 3.8 %while.1 = (s32[]{:T(128)}, f32[256,256]{1,0:T(8,128)S(1)}, s32[2,2]{1,0:T(2,128)S(1)}, f32[2,128,128]{2,1,0:T(8,128)S(1)}, s32[]{:T(128)}) while((s32[]{:T(128)}, f32[256,256]{1,0:T(8,128)S(1)}, s32[2,2]{1,0:T(2,128)S(1)}, f32[2,128,128]{2,1,0:T(8,128)S(1)}, s32[]{:T(128)}) %tuple.33), condition=%wide.while_cond, body=%wide.while_body.sunk | while | flops 2 | bytes 131189 | solution.py:93
  134.9 0.6 fusion.27
  135.5 1.3 bitcast_dynamic-update-slice_fusion.2
  136.8 0.6 fusion.27
  137.4 1.3 bitcast_dynamic-update-slice_fusion.2
  138.7 19.7 %custom-call.15 = f32[2,128,128]{1,2,0:T(8,128)S(1)} custom-call(f32[2,128,128]{2,1,0:T(8,128)S(1)} %get-tuple-element.9), custom_call_target="InvertDiagBlocksLowerTriangular" | custom-call | tf_op jit(solution)/shard_map/triangular_solve | solution.py:93
  159.1 0.6 pad_maximum_fusion
  (26 shorter events, 1.4 us)
Async XLA Ops:
  0.6 1.0 copy-start
  53.1 17.8 %all-to-all-start.2 = ((f32[64,1,128]{2,1,0:T(1,128)}), f32[64,1,128]{2,1,0:T(1,128)S(1)}, u32[]{:S(2)}, u32[]{:S(2)}) async-start(f32[64,1,128]{2,1,0:T(1,128)} %broadcast_in_dim.8), calls=%async_computation.2 | async-start | bytes 65536 | tf_op jit(solution)/shard_map/all_to_all | solution.py:38
  71.6 15.3 %all-to-all-start.3 = ((f32[8,64,128]{2,1,0:T(8,128)}), f32[8,64,128]{2,1,0:T(8,128)S(1)}, u32[]{:S(2)}, u32[]{:S(2)}) async-start(f32[8,64,128]{2,1,0:T(8,128)} %broadcast_in_dim.9), calls=%async_computation.3 | async-start | bytes 524288 | tf_op jit(solution)/shard_map/all_to_all | solution.py:38
  86.9 41.9 %all-to-all-start.4 = ((f32[8,64,2,256]{3,2,1,0:T(2,128)}), f32[8,64,2,256]{3,2,1,0:T(2,128)S(1)}, u32[]{:S(2)}, u32[]{:S(2)}) async-start(f32[8,64,2,256]{3,2,1,0:T(2,128)} %copy.25), calls=%async_computation.4 | async-start | bytes 2097152 | tf_op jit(solution)/shard_map/all_to_all | solution.py:17
  129.9 28.5 %all-to-all-start.5 = ((f32[64,2,256]{2,1,0:T(2,128)}), f32[64,2,256]{2,1,0:T(2,128)S(1)}, u32[]{:S(2)}, u32[]{:S(2)}) async-start(f32[64,2,256]{2,1,0:T(2,128)} %reduce_sum.38), calls=%async_computation.5 | async-start | bytes 262144 | tf_op jit(solution)/shard_map/all_to_all | solution.py:25
where the time goes:
time: 160 us
  other arithmetic  55.6 us (35%)
  blocking collectives  43.6 us (27%)
  starting transfers between devices  21.3 us (13%)
  matrix products  17.2 us (11%)
  local copies, waits for them, and re-layouts  11.1 us (7%)
  waiting for transfers between devices  8.79 us (5%)
  between operations  2.1 us (1%)
    another operation x6, other arithmetic, body(): lower = jnp.linalg.cholesky(total_gram)  33.9 us
    all_to_all x1, blocking collectives, sum_by_axis(): lax.all_to_all(nearer, far, split_axis=0, concat_axis=0, tiled=True)  27.9 us
    another operation x4, other arithmetic, body(): lax.linalg.triangular_solve(lower, cross, left_side=False, lower=True, tr...  20.3 us
    all_to_all x1, blocking collectives, sent_and_summed(): lax.all_to_all(pieces, axis, split_axis=0, concat_axis=0, tiled=True)  15.7 us
    all_to_all x2, starting transfers between devices, from_everyone(): return lax.all_to_all(copies, axis, split_axis=0, concat_axis=0, tiled=True)  11.5 us
    all_to_all x2, waiting for transfers between devices, from_everyone(): return lax.all_to_all(copies, axis, split_axis=0, concat_axis=0, tiled=True)  8.78 us
    all_to_all x1, starting transfers between devices, sum_by_axis(): lax.all_to_all(nearer, far, split_axis=0, concat_axis=0, tiled=True)  4.92 us
    all_to_all x1, starting transfers between devices, sent_and_summed(): lax.all_to_all(pieces, axis, split_axis=0, concat_axis=0, tiled=True)  4.83 us
  transfers between devices with their start and end apart: 4, of which 1 were waited for; matrix products, arithmetic and copies ran while one was open for 45% of the time, Pallas kernels for 0%

commit v1 on v0

v1 whole, which is shorter than its diff:
```python
import functools

import jax
import jax.numpy as jnp
import numpy as np
from jax import lax
from jax.experimental import pallas as pl
from jax.experimental.pallas import tpu as pltpu
from jax.sharding import Mesh
from jax.sharding import PartitionSpec as P

NT = (((1,), (1,)), ((), ()))
def nt(a,b): return lax.dot_general(a,b,NT,precision=lax.Precision.HIGHEST,preferred_element_type=jnp.float32)

def lanes(v, k):
    return jnp.broadcast_to(v[:, k:k+1], (8, 128))
def rows(v, t):
    return jnp.broadcast_to(v[t:t+1, :], (8, 128))

def factor128(a):
    lane = lax.broadcasted_iota(jnp.int32, (8, 128), 1)
    sub = lax.broadcasted_iota(jnp.int32, (8, 128), 0)
    a = list(a)
    w = [jnp.where(lane == sub + 8*i, 1.0, 0.0) for i in range(16)]
    for j in range(0, 128, 2):
        b, t = divmod(j, 8)
        r0, r1 = rows(a[b], t), rows(a[b], t+1)
        w0, w1 = rows(w[b], t), rows(w[b], t+1)
        p, q, s = lanes(r0, j), lanes(r0, j+1), lanes(r1, j+1)
        inv = 1.0 / (p*s - q*q)
        pi, qi, si = p*inv, q*inv, s*inv
        u0, u1 = si*r0 - qi*r1, pi*r1 - qi*r0
        v0, v1 = si*w0 - qi*w1, pi*w1 - qi*w0
        for i in range(b, 16):
            if i == b and t == 6: continue
            c0, c1 = lanes(a[i], j), lanes(a[i], j+1)
            if i == b:
                m = sub > t+1
                c0, c1 = jnp.where(m, c0, 0.0), jnp.where(m, c1, 0.0)
            a[i] = a[i] - (c0*u0 + c1*u1)
            w[i] = w[i] - (c0*v0 + c1*v1)
    ro, wo = [], []
    odd = sub % 2 == 1
    for i in range(16):
        d = lane - (sub + 8*i)
        p = jnp.sum(jnp.where(d == 0, a[i], 0.0), axis=1, keepdims=True)
        q = jnp.sum(jnp.where(d == 1, a[i], 0.0), axis=1, keepdims=True)
        f = jnp.broadcast_to(q / p, (8, 128))
        f = jnp.where(odd, pltpu.roll(f, 1, 0), 0.0)
        x = a[i] - f*pltpu.roll(a[i], 1, 0)
        y = w[i] - f*pltpu.roll(w[i], 1, 0)
        p = jnp.sum(jnp.where(d == 0, x, 0.0), axis=1, keepdims=True)
        g = jnp.broadcast_to(lax.rsqrt(p), (8, 128))
        ro.append(jnp.where(d >= 0, x*g, 0.0))
        wo.append(y*g)
    return ro, wo

def blocks(x): return [x[8*i:8*i+8, :] for i in range(x.shape[0]//8)]
def cat(bs): return jnp.concatenate(bs, axis=0)

def chol_kernel(scale, g_ref, c_ref, r_ref, p_ref):
    lane = lax.broadcasted_iota(jnp.int32, (128, 128), 1)
    sub = lax.broadcasted_iota(jnp.int32, (128, 128), 0)
    eye = lane == sub
    a11, a21, a22 = g_ref[0:128, :], g_ref[128:256, :], g_ref[256:384, :]
    def diag(x):
        e = jnp.where(eye, x, 0.0)
        return jnp.sum(e, axis=0, keepdims=True), jnp.sum(e, axis=1, keepdims=True)
    l1, s1 = diag(a11); l2, s2 = diag(a22)
    il1, is1, il2, is2 = map(lax.rsqrt, (l1, s1, l2, s2))
    c1, c2 = c_ref[0:8, :] * il1, pltpu.roll(c_ref[...], 6, 0) * il2
    a11 = a11 * is1 * il1
    a21 = a21 * is2 * il1
    a22 = a22 * is2 * il2
    r11, w1 = factor128(blocks(a11))
    r_ref[0:128, 0:128] = cat(r11) * (l1 * il1 * scale)
    w1 = cat(w1)
    low = nt(cat([a21, c1]), w1)
    l21, p1 = low[0:128], low[128:136]
    r_ref[0:128, 128:256] = nt(w1, a21) * (l2 * il2 * scale)
    upd = nt(low, l21)
    a22 = a22 - upd[0:128]
    c2 = c2 - upd[128:136]
    r22, w2 = factor128(blocks(a22))
    p2 = nt(c2, cat(w2))
    r_ref[128:256, 0:128] = jnp.zeros((128, 128), jnp.float32)
    r_ref[128:256, 128:256] = cat(r22) * (l2 * il2 * scale)
    p_ref[:, 0:128] = p1[0:2]
    p_ref[:, 128:256] = p2[0:2]

def chol(g, c, scale, **kw):
    return pl.pallas_call(functools.partial(chol_kernel, scale),
        out_shape=(jax.ShapeDtypeStruct((256,256),jnp.float32), jax.ShapeDtypeStruct((2,256),jnp.float32)), **kw)(g, c)

TN_NT = (((0,), (1,)), ((), ()))
GRAM_ROWS = 24
CROSS_ROWS = 64
PLANE = 16
RING = 16


def front_kernel(core_ref, deform_ref, sketch_ref, keep_ref, send_ref, cross_acc, gram_acc, lines):
    step = pl.program_id(0)
    deform = deform_ref[...]
    sketched = lax.dot_general(sketch_ref[...], deform, TN_NT, preferred_element_type=jnp.float32)
    high = sketched.astype(jnp.bfloat16)
    rest = (sketched - high.astype(jnp.float32)).astype(jnp.bfloat16)
    pair = jnp.concatenate([high, rest], axis=0)
    cross = jnp.dot(pair, deform, preferred_element_type=jnp.float32)
    cross = cross[:256] + cross[256:]
    gram = lax.dot_general(pair, high, NT, preferred_element_type=jnp.float32)

    @pl.when(step == 0)
    def _():
        cross_acc[...] = cross
        gram_acc[...] = gram

    @pl.when(step > 0)
    def _():
        cross_acc[...] += cross
        gram_acc[...] += gram

    @pl.when(step == pl.num_programs(0) - 1)
    def _():
        mixed = gram_acc[256:512, :]
        whole = gram_acc[0:256, :] + mixed + mixed.T
        packed = jnp.concatenate([whole[0:128, 0:128], whole[128:256, 0:128], whole[128:256, 128:256]], axis=0)
        for peer in range(PLANE):
            part = packed[peer * GRAM_ROWS : (peer + 1) * GRAM_ROWS]
            keep_ref[peer, 0:GRAM_ROWS, :] = part
            send_ref[peer, 0:GRAM_ROWS, :] = part
        for half in range(2):
            for block in range(8):
                tile = cross_acc[half * 128 : half * 128 + 128, block * 128 : block * 128 + 128]
                lines[half, block * 128 : block * 128 + 128, :] = tile.T
        core = core_ref[0]
        for peer in range(PLANE):
            y, x = divmod(peer, 4)
            for half in range(2):
                for i in range(2):
                    at = GRAM_ROWS + (half * 2 + i) * RING
                    base = y * 256 + x * 4 + i
                    keep_ref[peer, at : at + RING, :] = lines[half, pl.ds(base + core * 2, RING, stride=16), :]
                    send_ref[peer, at : at + RING, :] = lines[half, pl.ds(base + 2 - core * 2, RING, stride=16), :]


def front(deform, sketch, core, rows=2048):
    shape = jax.ShapeDtypeStruct((PLANE, GRAM_ROWS + CROSS_ROWS, 128), jnp.float32)
    whole = lambda *_: (0, 0, 0)
    return pl.pallas_call(
        front_kernel,
        grid_spec=pltpu.PrefetchScalarGridSpec(
            num_scalar_prefetch=1,
            grid=(deform.shape[0] // rows,),
            in_specs=[pl.BlockSpec((rows, 1024), lambda i, _: (i, 0)), pl.BlockSpec((1024, 256), lambda i, _: (0, 0))],
            out_specs=[pl.BlockSpec(shape.shape, whole)] * 2,
            scratch_shapes=[
                pltpu.VMEM((256, 1024), jnp.float32),
                pltpu.VMEM((512, 256), jnp.float32),
                pltpu.VMEM((2, 1024, 128), jnp.float32),
            ],
        ),
        out_shape=(shape, shape),
        compiler_params=pltpu.CompilerParams(vmem_limit_bytes=60 << 20),
        name="front",
    )(core, deform, sketch)


def plane_kernel(in_ref, out_ref):
    total = in_ref[0]
    for peer in range(1, PLANE):
        total = total + in_ref[peer]
    spare = jnp.zeros((4, 128), jnp.float32)
    for z in range(RING):
        out_ref[z * 32 : z * 32 + GRAM_ROWS, :] = total[0:GRAM_ROWS]
        out_ref[z * 32 + 28 : z * 32 + 32, :] = spare
    for q in range(4):
        at = GRAM_ROWS + q * RING
        out_ref[pl.ds(GRAM_ROWS + q, RING, stride=32), :] = total[at : at + RING]


def plane_sum(arrived):
    out = pl.pallas_call(
        plane_kernel,
        out_shape=jax.ShapeDtypeStruct((RING * 32, 128), jnp.float32),
        name="plane_sum",
    )(arrived)
    return out.reshape(RING, 32, 128)


def ring_kernel(in_ref, chunk_ref, own_ref):
    total = in_ref[0]
    for z in range(1, RING):
        total = total + in_ref[z]
    for peer in range(PLANE):
        chunk_ref[peer] = total[0:GRAM_ROWS]
    own_ref[...] = total[GRAM_ROWS:32]


def ring_sum(arrived):
    return pl.pallas_call(
        ring_kernel,
        out_shape=(
            jax.ShapeDtypeStruct((PLANE, GRAM_ROWS, 128), jnp.float32),
            jax.ShapeDtypeStruct((8, 128), jnp.float32),
        ),
        name="ring_sum",
    )(arrived)


def swap(values, axis):
    return lax.all_to_all(values, axis, split_axis=0, concat_axis=0, tiled=True)


def body(deform, sketch):
    core = lax.axis_index("c").astype(jnp.int32).reshape(1)
    keep, send = front(deform, sketch, core)
    chip = keep + lax.ppermute(send, "c", [(0, 1), (1, 0)])
    own_plane = plane_sum(swap(chip, ("y", "x")))
    chunks, own = ring_sum(swap(own_plane, ("z",)))
    packed = swap(chunks, ("y", "x")).reshape(384, 128)
    total_rows = deform.shape[0] * lax.axis_size(("y", "z", "x", "c"))
    return chol(packed, own, 1.0 / float(np.sqrt(np.float32(total_rows))))


def solution(mesh):
    split = Mesh(mesh.devices.reshape(4, 16, 4, 2), ("y", "z", "x", "c"))
    axes = ("y", "z", "x", "c")
    in_specs = (P(axes, None), P())
    out_specs = (P(), P(axes, None))
    return jax.shard_map(body, mesh=split, in_specs=in_specs, out_specs=out_specs, check_vma=False)
```

time: 160 us -> 106 us (0.66)
  the two profiles are of different devices: /device:TPU:1 before, /device:TPU:32 now
where the time goes in v1:
time: 106 us; the launch traced here: 105 us
  blocking collectives  66.2 us (62%)
  Pallas kernels  32.7 us (31%)
  waiting for transfers between devices  2.37 us (2%)
  starting transfers between devices  1.91 us (2%)
  other arithmetic  1.18 us (1%)
    all_to_all x3, blocking collectives, swap(): return lax.all_to_all(values, axis, split_axis=0, concat_axis=0, tiled=True)  66.2 us
    pallas_call x1, Pallas kernels, chol(): pl.pallas_call(functools.partial(chol_kernel, scale), out_shape=(jax.Shap...  21.4 us
    pallas_call x1, Pallas kernels, front(): pl.pallas_call(front_kernel, grid_spec=pltpu.PrefetchScalarGridSpec(num_s...  7.77 us
    ppermute x1, waiting for transfers between devices, body(): chip = keep + lax.ppermute(send, 'c', [(0, 1), (1, 0)])  2.37 us
  transfers between devices with their start and end apart: 1, of which 1 were waited for; matrix products, arithmetic and copies ran while one was open for 0% of the time, Pallas kernels for 0%

profile of v1, /device:TPU:32, one launch (start us, length us, event | category | flops | bytes accessed | tf_op | source)
XLA Modules:
  0.0 105.0 jit_solution(14586428204730517931)
XLA Ops:
  0.6 7.8 %front.1 = (f32[16,88,128]{2,1,0:T(8,128)}, f32[16,88,128]{2,1,0:T(8,128)}) custom-call(s32[1]{0:T(128)} %bitcast.core_ref, bf16[2048,1024]{1,0:T(8,128)(2,1)} %deform_ref.1, bf16[1024,256]{1,0:T(8,128)(2,1)} %sketch_ref.1), custom_call_target="tpu_custom_call" | custom-call | tf_op jit(solution)/shard_map/front/pallas_call | solution.py:150
  8.4 1.9 %collective-permute-start = (f32[16,88,128]{2,1,0:T(8,128)}, f32[16,88,128]{2,1,0:T(8,128)S(1)}, u32[]{:S(2)}, u32[]{:S(2)}) collective-permute-start(f32[16,88,128]{2,1,0:T(8,128)} %get-tuple-element.7), channel_id=1, source_target_pairs={{0,1},{1,0},{2,3},{3,2},{4,5},{5,4},{6,7},{7,6},{8,9},{9,8},{10,11... | collective-permute-start | bytes 2162696 | tf_op jit(solution)/shard_map/ppermute | solution.py:218
  10.3 2.4 %collective-permute-done = f32[16,88,128]{2,1,0:T(8,128)S(1)} collective-permute-done((f32[16,88,128]{2,1,0:T(8,128)}, f32[16,88,128]{2,1,0:T(8,128)S(1)}, u32[]{:S(2)}, u32[]{:S(2)}) %collective-permute-start) | collective-permute-done | bytes 720928 | tf_op jit(solution)/shard_map/ppermute | solution.py:218
  12.7 1.2 %add.3 = f32[16,88,128]{2,1,0:T(8,128)S(1)} add(f32[16,88,128]{2,1,0:T(8,128)} %get-tuple-element.6, f32[16,88,128]{2,1,0:T(8,128)S(1)} %collective-permute-done) | non-fusion elementwise | flops 180224 | bytes 2162688 | tf_op jit(solution)/shard_map/add | solution.py:218
  13.9 20.9 %all_to_all.15.in_ref = f32[16,88,128]{2,1,0:T(8,128)} all-to-all(f32[16,88,128]{2,1,0:T(8,128)S(1)} %add.3), channel_id=1, replica_groups=mesh['y'=4,'z'=16,'x'=4,'c'=2] {'y','x'}, dimensions={0} | all-to-all | bytes 1441792 | tf_op jit(solution)/shard_map/all_to_all | solution.py:212
  34.8 1.9 %plane_sum.1 = f32[512,128]{1,0:T(8,128)} custom-call(f32[16,88,128]{2,1,0:T(8,128)} %all_to_all.15.in_ref), custom_call_target="tpu_custom_call" | custom-call | tf_op jit(solution)/shard_map/plane_sum/pallas_call | solution.py:183
  36.6 32.8 %all_to_all.16.in_ref = f32[16,32,128]{2,1,0:T(8,128)} all-to-all(f32[16,32,128]{2,1,0:T(8,128)} %bitcast.3), channel_id=1, replica_groups=mesh['y'=4,'z'=16,'x'=4,'c'=2] {'z'}, dimensions={0} | all-to-all | bytes 524288 | tf_op jit(solution)/shard_map/all_to_all | solution.py:212
  69.5 1.7 %ring_sum.1 = (f32[16,24,128]{2,1,0:T(8,128)}, f32[8,128]{1,0:T(8,128)}) custom-call(f32[16,32,128]{2,1,0:T(8,128)} %all_to_all.16.in_ref), custom_call_target="tpu_custom_call" | custom-call | tf_op jit(solution)/shard_map/ring_sum/pallas_call | solution.py:201
  71.1 12.5 %all_to_all.17 = f32[16,24,128]{2,1,0:T(8,128)} all-to-all(f32[16,24,128]{2,1,0:T(8,128)} %get-tuple-element.8), channel_id=1, replica_groups=mesh['y'=4,'z'=16,'x'=4,'c'=2] {'y','x'}, dimensions={0} | all-to-all | bytes 393216 | tf_op jit(solution)/shard_map/all_to_all | solution.py:212
  83.7 21.4 %shard_map.41 = (f32[256,256]{1,0:T(8,128)}, f32[2,256]{1,0:T(2,128)}) custom-call(f32[384,128]{1,0:T(8,128)} %bitcast.4, f32[8,128]{1,0:T(8,128)} %get-tuple-element.9.c_ref), custom_call_target="tpu_custom_call" | custom-call | tf_op jit(solution)/shard_map/pallas_call | solution.py:92
Async XLA Ops:
  8.4 4.3 %collective-permute-start = (f32[16,88,128]{2,1,0:T(8,128)}, f32[16,88,128]{2,1,0:T(8,128)S(1)}, u32[]{:S(2)}, u32[]{:S(2)}) collective-permute-start(f32[16,88,128]{2,1,0:T(8,128)} %get-tuple-element.7), channel_id=1, source_target_pairs={{0,1},{1,0},{2,3},{3,2},{4,5},{5,4},{6,7},{7,6},{8,9},{9,8},{10,11... | collective-permute-start | bytes 2162696 | tf_op jit(solution)/shard_map/ppermute | solution.py:218

commit v2 on v1

--- a/solution.py
+++ b/solution.py
@@ -22,23 +22,31 @@
     sub = lax.broadcasted_iota(jnp.int32, (8, 128), 0)
     a = list(a)
     w = [jnp.where(lane == sub + 8*i, 1.0, 0.0) for i in range(16)]
-    for j in range(0, 128, 2):
-        b, t = divmod(j, 8)
-        r0, r1 = rows(a[b], t), rows(a[b], t+1)
-        w0, w1 = rows(w[b], t), rows(w[b], t+1)
-        p, q, s = lanes(r0, j), lanes(r0, j+1), lanes(r1, j+1)
-        inv = 1.0 / (p*s - q*q)
-        pi, qi, si = p*inv, q*inv, s*inv
-        u0, u1 = si*r0 - qi*r1, pi*r1 - qi*r0
-        v0, v1 = si*w0 - qi*w1, pi*w1 - qi*w0
-        for i in range(b, 16):
-            if i == b and t == 6: continue
-            c0, c1 = lanes(a[i], j), lanes(a[i], j+1)
-            if i == b:
-                m = sub > t+1
-                c0, c1 = jnp.where(m, c0, 0.0), jnp.where(m, c1, 0.0)
-            a[i] = a[i] - (c0*u0 + c1*u1)
-            w[i] = w[i] - (c0*v0 + c1*v1)
+    fa, fw = [], []
+    for b in range(16):
+        x = [lanes(a[b], 8*b+k) for k in range(8)] + [a[b], w[b]]
+        f = [a[b], w[b]]
+        for t in range(0, 8, 2):
+            if t:
+                late = sub >= t
+                f = [jnp.where(late, n, o) for n, o in zip(x[8:], f)]
+            c0, c1 = x[t], x[t+1]
+            p, q, s = rows(c0, t), rows(c0, t+1), rows(c1, t+1)
+            inv = 1.0 / (p*s - q*q)
+            pi, qi, si = p*inv, q*inv, s*inv
+            for k in range(t+2, 10):
+                r0, r1 = rows(x[k], t), rows(x[k], t+1)
+                u0, u1 = si*r0 - qi*r1, pi*r1 - qi*r0
+                new = x[k] - (c0*u0 + c1*u1)
+                x[k] = jnp.where(sub == t, u0, jnp.where(sub == t+1, u1, new))
+        fa.append(f[0]); fw.append(f[1])
+        ga = [rows(x[8], k) for k in range(8)]
+        gw = [rows(x[9], k) for k in range(8)]
+        for i in range(b+1, 16):
+            c = [lanes(a[i], 8*b+k) for k in range(8)]
+            a[i] = a[i] - tree([c[k]*ga[k] for k in range(8)])
+            w[i] = w[i] - tree([c[k]*gw[k] for k in range(8)])
+    a, w = fa, fw
     ro, wo = [], []
     odd = sub % 2 == 1
     for i in range(16):
@@ -54,6 +62,10 @@
         ro.append(jnp.where(d >= 0, x*g, 0.0))
         wo.append(y*g)
     return ro, wo
+
+def tree(v):
+    while len(v) > 1: v = [v[n] + v[n+1] for n in range(0, len(v), 2)]
+    return v[0]
 
 def blocks(x): return [x[8*i:8*i+8, :] for i in range(x.shape[0]//8)]
 def cat(bs): return jnp.concatenate(bs, axis=0)
@@ -97,73 +109,72 @@
 CROSS_ROWS = 64
 PLANE = 16
 RING = 16
-
-
-def front_kernel(core_ref, deform_ref, sketch_ref, keep_ref, send_ref, cross_acc, gram_acc, lines):
-    step = pl.program_id(0)
-    deform = deform_ref[...]
-    sketched = lax.dot_general(sketch_ref[...], deform, TN_NT, preferred_element_type=jnp.float32)
-    high = sketched.astype(jnp.bfloat16)
-    rest = (sketched - high.astype(jnp.float32)).astype(jnp.bfloat16)
-    pair = jnp.concatenate([high, rest], axis=0)
-    cross = jnp.dot(pair, deform, preferred_element_type=jnp.float32)
-    cross = cross[:256] + cross[256:]
-    gram = lax.dot_general(pair, high, NT, preferred_element_type=jnp.float32)
-
-    @pl.when(step == 0)
-    def _():
-        cross_acc[...] = cross
-        gram_acc[...] = gram
-
-    @pl.when(step > 0)
-    def _():
-        cross_acc[...] += cross
-        gram_acc[...] += gram
-
-    @pl.when(step == pl.num_programs(0) - 1)
-    def _():
-        mixed = gram_acc[256:512, :]
-        whole = gram_acc[0:256, :] + mixed + mixed.T
-        packed = jnp.concatenate([whole[0:128, 0:128], whole[128:256, 0:128], whole[128:256, 128:256]], axis=0)
-        for peer in range(PLANE):
-            part = packed[peer * GRAM_ROWS : (peer + 1) * GRAM_ROWS]
-            keep_ref[peer, 0:GRAM_ROWS, :] = part
-            send_ref[peer, 0:GRAM_ROWS, :] = part
+ROWS = 2048
+CHUNKS = 4
+SMALL = pltpu.CompilerParams(vmem_limit_bytes=8 << 20)
+
+
+def front_kernel(core_ref, deform_hbm, sketch_hbm, keep_ref, send_ref, deform, sketch, pair, lines, sems):
+    span = ROWS // CHUNKS
+    load = pltpu.make_async_copy(sketch_hbm, sketch, sems.at[CHUNKS])
+    load.start()
+    loads = []
+    for n in range(CHUNKS):
+        part = pl.ds(n * span, span)
+        loads.append(pltpu.make_async_copy(deform_hbm.at[part], deform.at[part], sems.at[n]))
+        loads[-1].start()
+    load.wait()
+    for n in range(CHUNKS):
+        loads[n].wait()
+        part = slice(n * span, (n + 1) * span)
+        sketched = lax.dot_general(sketch[...], deform[part], TN_NT, preferred_element_type=jnp.float32)
+        high = sketched.astype(jnp.bfloat16)
+        pair[0:256, part] = high
+        pair[256:512, part] = (sketched - high.astype(jnp.float32)).astype(jnp.bfloat16)
+    gram = lax.dot_general(pair[...], pair[0:256, :], NT, preferred_element_type=jnp.float32)
+    mixed = gram[256:512]
+    whole = gram[0:256] + mixed + mixed.T
+    packed = jnp.concatenate([whole[0:128, 0:128], whole[128:256, 0:128], whole[128:256, 128:256]], axis=0)
+    for peer in range(PLANE):
+        part = packed[peer * GRAM_ROWS : (peer + 1) * GRAM_ROWS]
+        keep_ref[peer, 0:GRAM_ROWS, :] = part
+        send_ref[peer, 0:GRAM_ROWS, :] = part
+    core = core_ref[0]
+    for y in range(4):
+        cols = slice(y * 256, y * 256 + 256)
+        cross = jnp.dot(pair[...], deform[:, cols], preferred_element_type=jnp.float32)
+        cross = cross[0:256] + cross[256:512]
         for half in range(2):
-            for block in range(8):
-                tile = cross_acc[half * 128 : half * 128 + 128, block * 128 : block * 128 + 128]
-                lines[half, block * 128 : block * 128 + 128, :] = tile.T
-        core = core_ref[0]
-        for peer in range(PLANE):
-            y, x = divmod(peer, 4)
+            for block in range(2):
+                at = y * 256 + block * 128
+                tile = cross[half * 128 : half * 128 + 128, block * 128 : block * 128 + 128]
+                lines[half, at : at + 128, :] = tile.T
+        for x in range(4):
             for half in range(2):
                 for i in range(2):
                     at = GRAM_ROWS + (half * 2 + i) * RING
                     base = y * 256 + x * 4 + i
-                    keep_ref[peer, at : at + RING, :] = lines[half, pl.ds(base + core * 2, RING, stride=16), :]
-                    send_ref[peer, at : at + RING, :] = lines[half, pl.ds(base + 2 - core * 2, RING, stride=16), :]
-
-
-def front(deform, sketch, core, rows=2048):
+                    keep_ref[y * 4 + x, at : at + RING, :] = lines[half, pl.ds(base + core * 2, RING, stride=16), :]
+                    send_ref[y * 4 + x, at : at + RING, :] = lines[half, pl.ds(base + 2 - core * 2, RING, stride=16), :]
+
+
+def front(deform, sketch, core):
     shape = jax.ShapeDtypeStruct((PLANE, GRAM_ROWS + CROSS_ROWS, 128), jnp.float32)
-    whole = lambda *_: (0, 0, 0)
     return pl.pallas_call(
         front_kernel,
-        grid_spec=pltpu.PrefetchScalarGridSpec(
-            num_scalar_prefetch=1,
-            grid=(deform.shape[0] // rows,),
-            in_specs=[pl.BlockSpec((rows, 1024), lambda i, _: (i, 0)), pl.BlockSpec((1024, 256), lambda i, _: (0, 0))],
-            out_specs=[pl.BlockSpec(shape.shape, whole)] * 2,
-            scratch_shapes=[
-                pltpu.VMEM((256, 1024), jnp.float32),
-                pltpu.VMEM((512, 256), jnp.float32),
-                pltpu.VMEM((2, 1024, 128), jnp.float32),
-            ],
-        ),
+        in_specs=[pl.BlockSpec(memory_space=pltpu.SMEM)] + [pl.BlockSpec(memory_space=pltpu.HBM)] * 2,
+        out_specs=[pl.BlockSpec(memory_space=pltpu.VMEM)] * 2,
+        scratch_shapes=[
+            pltpu.VMEM((ROWS, 1024), jnp.bfloat16),
+            pltpu.VMEM((1024, 256), jnp.bfloat16),
+            pltpu.VMEM((512, ROWS), jnp.bfloat16),
+            pltpu.VMEM((2, 1024, 128), jnp.float32),
+            pltpu.SemaphoreType.DMA((CHUNKS + 1,)),
+        ],
         out_shape=(shape, shape),
-        compiler_params=pltpu.CompilerParams(vmem_limit_bytes=60 << 20),
+        compiler_params=pltpu.CompilerParams(vmem_limit_bytes=32 << 20),
         name="front",
-    )(core, deform, sketch)
+    )(core, pltpu.with_memory_space_constraint(deform, pltpu.HBM), pltpu.with_memory_space_constraint(sketch, pltpu.HBM))
 
 
 def plane_kernel(in_ref, out_ref):
@@ -183,6 +194,7 @@
     out = pl.pallas_call(
         plane_kernel,
         out_shape=jax.ShapeDtypeStruct((RING * 32, 128), jnp.float32),
+        compiler_params=SMALL,
         name="plane_sum",
     )(arrived)
     return out.reshape(RING, 32, 128)
@@ -204,6 +216,7 @@
             jax.ShapeDtypeStruct((PLANE, GRAM_ROWS, 128), jnp.float32),
             jax.ShapeDtypeStruct((8, 128), jnp.float32),
         ),
+        compiler_params=SMALL,
         name="ring_sum",
     )(arrived)
 
@@ -220,7 +233,7 @@
     chunks, own = ring_sum(swap(own_plane, ("z",)))
     packed = swap(chunks, ("y", "x")).reshape(384, 128)
     total_rows = deform.shape[0] * lax.axis_size(("y", "z", "x", "c"))
-    return chol(packed, own, 1.0 / float(np.sqrt(np.float32(total_rows))))
+    return chol(packed, own, 1.0 / float(np.sqrt(np.float32(total_rows))), compiler_params=SMALL, name="factor")
 
 
 def solution(mesh):

time: 106 us -> 87.6 us (0.83)
  Pallas kernels: 32.7 us -> 17.7 us
  blocking collectives: 66.2 us -> 64.8 us
  other arithmetic: 1.18 us -> 0.11 us
    pallas_call x1, Pallas kernels: 21.4 us -> 11.2 us  [chol(): pl.pallas_call(functools.partial(chol_kernel, scale), out_shape=(jax.Shap...]
    pallas_call x1, Pallas kernels: 1.89 us -> 0.07 us  [plane_sum(): pl.pallas_call(plane_kernel, out_shape=jax.ShapeDtypeStruct((RING * 32, 1...]
    pallas_call x1, Pallas kernels: 1.66 us -> 0.03 us  [ring_sum(): pl.pallas_call(ring_kernel, out_shape=(jax.ShapeDtypeStruct((PLANE, GRAM_...]
    pallas_call x1, Pallas kernels: 7.77 us -> 6.38 us  [front(): pl.pallas_call(front_kernel, in_specs=[pl.BlockSpec(memory_space=pltpu.SM...]
    all_to_all x3, blocking collectives: 66.2 us -> 64.8 us  [swap(): return lax.all_to_all(values, axis, split_axis=0, concat_axis=0, tiled=True)]
    add x1, other arithmetic: 1.18 us -> 0.11 us  [body(): chip = keep + lax.ppermute(send, 'c', [(0, 1), (1, 0)])]
where the time goes in v2:
time: 87.6 us; the launch traced here: 87.4 us
  blocking collectives  64.8 us (74%)
  Pallas kernels  17.7 us (20%)
  waiting for transfers between devices  2.16 us (2%)
  starting transfers between devices  1.92 us (2%)
    all_to_all x3, blocking collectives, swap(): return lax.all_to_all(values, axis, split_axis=0, concat_axis=0, tiled=True)  64.8 us
    pallas_call x1, Pallas kernels, chol(): pl.pallas_call(functools.partial(chol_kernel, scale), out_shape=(jax.Shap...  11.2 us
    pallas_call x1, Pallas kernels, front(): pl.pallas_call(front_kernel, in_specs=[pl.BlockSpec(memory_space=pltpu.SM...  6.38 us
    ppermute x1, waiting for transfers between devices, body(): chip = keep + lax.ppermute(send, 'c', [(0, 1), (1, 0)])  2.16 us
    ppermute x1, starting transfers between devices, body(): chip = keep + lax.ppermute(send, 'c', [(0, 1), (1, 0)])  1.92 us
  transfers between devices with their start and end apart: 1, of which 1 were waited for; matrix products, arithmetic and copies ran while one was open for 0% of the time, Pallas kernels for 0%

profile of v2, /device:TPU:32, one launch (start us, length us, event | category | flops | bytes accessed | tf_op | source)
XLA Modules:
  0.0 87.4 jit_solution(14666828762014564551)
XLA Ops:
  0.6 6.4 %front.1 = (f32[16,88,128]{2,1,0:T(8,128)S(1)}, f32[16,88,128]{2,1,0:T(8,128)S(1)}) custom-call(s32[1]{0:T(128)} %bitcast.core_ref, bf16[2048,1024]{1,0:T(8,128)(2,1)} %deform_hbm.1, bf16[1024,256]{1,0:T(8,128)(2,1)} %sketch_hbm.1), custom_call_target="tpu_custom_call" | custom-call | tf_op jit(solution)/shard_map/front/pallas_call | solution.py:163
  7.0 1.9 %collective-permute-start = (f32[16,88,128]{2,1,0:T(8,128)S(1)}, f32[16,88,128]{2,1,0:T(8,128)S(1)}, u32[]{:S(2)}, u32[]{:S(2)}) collective-permute-start(f32[16,88,128]{2,1,0:T(8,128)S(1)} %get-tuple-element.7), channel_id=1, source_target_pairs={{0,1},{1,0},{2,3},{3,2},{4,5},{5,4},{6,7},{7,6},{8,9},{9,8},{10,11... | collective-permute-start | bytes 2162696 | tf_op jit(solution)/shard_map/ppermute | solution.py:231
  8.9 2.2 %collective-permute-done = f32[16,88,128]{2,1,0:T(8,128)S(1)} collective-permute-done((f32[16,88,128]{2,1,0:T(8,128)S(1)}, f32[16,88,128]{2,1,0:T(8,128)S(1)}, u32[]{:S(2)}, u32[]{:S(2)}) %collective-permute-start) | collective-permute-done | bytes 720928 | tf_op jit(solution)/shard_map/ppermute | solution.py:231
  11.1 0.1 add.3
  11.2 20.8 %all_to_all.15.in_ref = f32[16,88,128]{2,1,0:T(8,128)S(1)} all-to-all(f32[16,88,128]{2,1,0:T(8,128)S(1)} %add.3), channel_id=1, replica_groups=mesh['y'=4,'z'=16,'x'=4,'c'=2] {'y','x'}, dimensions={0} | all-to-all | bytes 1441792 | tf_op jit(solution)/shard_map/all_to_all | solution.py:225
  32.0 0.1 plane_sum.1
  32.1 32.5 %all_to_all.16.in_ref = f32[16,32,128]{2,1,0:T(8,128)S(1)} all-to-all(f32[16,32,128]{2,1,0:T(8,128)S(1)} %bitcast.3), channel_id=1, replica_groups=mesh['y'=4,'z'=16,'x'=4,'c'=2] {'z'}, dimensions={0} | all-to-all | bytes 524288 | tf_op jit(solution)/shard_map/all_to_all | solution.py:225
  64.6 11.5 %all_to_all.17 = f32[16,24,128]{2,1,0:T(8,128)S(1)} all-to-all(f32[16,24,128]{2,1,0:T(8,128)S(1)} %get-tuple-element.8), channel_id=1, replica_groups=mesh['y'=4,'z'=16,'x'=4,'c'=2] {'y','x'}, dimensions={0} | all-to-all | bytes 393216 | tf_op jit(solution)/shard_map/all_to_all | solution.py:225
  76.2 11.2 %factor.1 = (f32[256,256]{1,0:T(8,128)}, f32[2,256]{1,0:T(2,128)}) custom-call(f32[384,128]{1,0:T(8,128)S(1)} %bitcast.4, f32[8,128]{1,0:T(8,128)S(1)} %get-tuple-element.9.c_ref), custom_call_target="tpu_custom_call" | custom-call | tf_op jit(solution)/shard_map/factor/pallas_call | solution.py:104
  (1 shorter events, 0.0 us)
Async XLA Ops:
  7.0 4.1 %collective-permute-start = (f32[16,88,128]{2,1,0:T(8,128)S(1)}, f32[16,88,128]{2,1,0:T(8,128)S(1)}, u32[]{:S(2)}, u32[]{:S(2)}) collective-permute-start(f32[16,88,128]{2,1,0:T(8,128)S(1)} %get-tuple-element.7), channel_id=1, source_target_pairs={{0,1},{1,0},{2,3},{3,2},{4,5},{5,4},{6,7},{7,6},{8,9},{9,8},{10,11... | collective-permute-start | bytes 2162696 | tf_op jit(solution)/shard_map/ppermute | solution.py:231

commit v3 on v2

--- a/solution.py
+++ b/solution.py
@@ -23,45 +23,42 @@
     a = list(a)
     w = [jnp.where(lane == sub + 8*i, 1.0, 0.0) for i in range(16)]
     fa, fw = [], []
+    todo = []
     for b in range(16):
-        x = [lanes(a[b], 8*b+k) for k in range(8)] + [a[b], w[b]]
-        f = [a[b], w[b]]
+        x = [jnp.where(lane < 128 + k, lanes(a[b], 8*b+k), 1.0) for k in range(8)] + [a[b], w[b]]
+        f = [None, None]
+        share = -(-len(todo) // 4)
         for t in range(0, 8, 2):
-            if t:
-                late = sub >= t
-                f = [jnp.where(late, n, o) for n, o in zip(x[8:], f)]
             c0, c1 = x[t], x[t+1]
             p, q, s = rows(c0, t), rows(c0, t+1), rows(c1, t+1)
-            inv = 1.0 / (p*s - q*q)
+            det = p*s - q*q
+            inv = 1.0 / det
+            g0 = lax.rsqrt(p)
+            g1 = p * lax.rsqrt(p * det)
+            step = q * g0 * g0
             pi, qi, si = p*inv, q*inv, s*inv
             for k in range(t+2, 10):
                 r0, r1 = rows(x[k], t), rows(x[k], t+1)
+                if k >= 8:
+                    y0, y1 = r0*g0, (r1 - step*r0)*g1
+                    f[k-8] = jnp.where(sub == t, y0, y1) if t == 0 else jnp.where(sub < t, f[k-8], jnp.where(sub == t, y0, y1))
                 u0, u1 = si*r0 - qi*r1, pi*r1 - qi*r0
                 new = x[k] - (c0*u0 + c1*u1)
                 x[k] = jnp.where(sub == t, u0, jnp.where(sub == t+1, u1, new))
+            for work in todo[:share]: work()
+            todo = todo[share:]
+        for work in todo: work()
         fa.append(f[0]); fw.append(f[1])
         ga = [rows(x[8], k) for k in range(8)]
         gw = [rows(x[9], k) for k in range(8)]
-        for i in range(b+1, 16):
+        def update(i, b=b, ga=ga, gw=gw):
             c = [lanes(a[i], 8*b+k) for k in range(8)]
             a[i] = a[i] - tree([c[k]*ga[k] for k in range(8)])
             w[i] = w[i] - tree([c[k]*gw[k] for k in range(8)])
-    a, w = fa, fw
-    ro, wo = [], []
-    odd = sub % 2 == 1
-    for i in range(16):
-        d = lane - (sub + 8*i)
-        p = jnp.sum(jnp.where(d == 0, a[i], 0.0), axis=1, keepdims=True)
-        q = jnp.sum(jnp.where(d == 1, a[i], 0.0), axis=1, keepdims=True)
-        f = jnp.broadcast_to(q / p, (8, 128))
-        f = jnp.where(odd, pltpu.roll(f, 1, 0), 0.0)
-        x = a[i] - f*pltpu.roll(a[i], 1, 0)
-        y = w[i] - f*pltpu.roll(w[i], 1, 0)
-        p = jnp.sum(jnp.where(d == 0, x, 0.0), axis=1, keepdims=True)
-        g = jnp.broadcast_to(lax.rsqrt(p), (8, 128))
-        ro.append(jnp.where(d >= 0, x*g, 0.0))
-        wo.append(y*g)
-    return ro, wo
+        if b < 15: update(b+1)
+        todo = [functools.partial(update, i) for i in range(b+2, 16)]
+    ro = [jnp.where(lane >= sub + 8*i, fa[i], 0.0) for i in range(16)]
+    return ro, fw
 
 def tree(v):
     while len(v) > 1: v = [v[n] + v[n+1] for n in range(0, len(v), 2)]
@@ -104,17 +101,16 @@
     return pl.pallas_call(functools.partial(chol_kernel, scale),
         out_shape=(jax.ShapeDtypeStruct((256,256),jnp.float32), jax.ShapeDtypeStruct((2,256),jnp.float32)), **kw)(g, c)
 
-TN_NT = (((0,), (1,)), ((), ()))
 GRAM_ROWS = 24
 CROSS_ROWS = 64
 PLANE = 16
 RING = 16
 ROWS = 2048
-CHUNKS = 4
+CHUNKS = 2
 SMALL = pltpu.CompilerParams(vmem_limit_bytes=8 << 20)
 
 
-def front_kernel(core_ref, deform_hbm, sketch_hbm, keep_ref, send_ref, deform, sketch, pair, lines, sems):
+def front_kernel(core_ref, deform_hbm, sketch_hbm, keep_ref, send_ref, deform, sketch, pair, lines, flat, sems):
     span = ROWS // CHUNKS
     load = pltpu.make_async_copy(sketch_hbm, sketch, sems.at[CHUNKS])
     load.start()
@@ -124,10 +120,11 @@
         loads.append(pltpu.make_async_copy(deform_hbm.at[part], deform.at[part], sems.at[n]))
         loads[-1].start()
     load.wait()
+    flat[...] = sketch[...].T
     for n in range(CHUNKS):
         loads[n].wait()
         part = slice(n * span, (n + 1) * span)
-        sketched = lax.dot_general(sketch[...], deform[part], TN_NT, preferred_element_type=jnp.float32)
+        sketched = lax.dot_general(flat[...], deform[part], NT, preferred_element_type=jnp.float32)
         high = sketched.astype(jnp.bfloat16)
         pair[0:256, part] = high
         pair[256:512, part] = (sketched - high.astype(jnp.float32)).astype(jnp.bfloat16)
@@ -169,6 +166,7 @@
             pltpu.VMEM((1024, 256), jnp.bfloat16),
             pltpu.VMEM((512, ROWS), jnp.bfloat16),
             pltpu.VMEM((2, 1024, 128), jnp.float32),
+            pltpu.VMEM((256, 1024), jnp.bfloat16),
             pltpu.SemaphoreType.DMA((CHUNKS + 1,)),
         ],
         out_shape=(shape, shape),

time: 87.6 us -> 84.7 us (0.967)
  Pallas kernels: 17.7 us -> 14.8 us
    pallas_call x1, Pallas kernels: 11.2 us -> 8.34 us  [chol(): pl.pallas_call(functools.partial(chol_kernel, scale), out_shape=(jax.Shap...]
where the time goes in v3:
time: 84.7 us; the launch traced here: 84.5 us
  blocking collectives  64.9 us (77%)
  Pallas kernels  14.8 us (17%)
  waiting for transfers between devices  2.16 us (3%)
  starting transfers between devices  1.92 us (2%)
    all_to_all x3, blocking collectives, swap(): return lax.all_to_all(values, axis, split_axis=0, concat_axis=0, tiled=True)  64.9 us
    pallas_call x1, Pallas kernels, chol(): pl.pallas_call(functools.partial(chol_kernel, scale), out_shape=(jax.Shap...  8.34 us
    pallas_call x1, Pallas kernels, front(): pl.pallas_call(front_kernel, in_specs=[pl.BlockSpec(memory_space=pltpu.SM...  6.32 us
    ppermute x1, waiting for transfers between devices, body(): chip = keep + lax.ppermute(send, 'c', [(0, 1), (1, 0)])  2.16 us
    ppermute x1, starting transfers between devices, body(): chip = keep + lax.ppermute(send, 'c', [(0, 1), (1, 0)])  1.92 us
  transfers between devices with their start and end apart: 1, of which 1 were waited for; matrix products, arithmetic and copies ran while one was open for 0% of the time, Pallas kernels for 0%

profile of v3, /device:TPU:32, one launch (start us, length us, event | category | flops | bytes accessed | tf_op | source)
XLA Modules:
  0.0 84.5 jit_solution(3320946008602966076)
XLA Ops:
  0.6 6.3 %front.1 = (f32[16,88,128]{2,1,0:T(8,128)S(1)}, f32[16,88,128]{2,1,0:T(8,128)S(1)}) custom-call(s32[1]{0:T(128)} %bitcast.core_ref, bf16[2048,1024]{1,0:T(8,128)(2,1)} %deform_hbm.1, bf16[1024,256]{1,0:T(8,128)(2,1)} %sketch_hbm.1), custom_call_target="tpu_custom_call" | custom-call | tf_op jit(solution)/shard_map/front/pallas_call | solution.py:160
  7.0 1.9 %collective-permute-start = (f32[16,88,128]{2,1,0:T(8,128)S(1)}, f32[16,88,128]{2,1,0:T(8,128)S(1)}, u32[]{:S(2)}, u32[]{:S(2)}) collective-permute-start(f32[16,88,128]{2,1,0:T(8,128)S(1)} %get-tuple-element.7), channel_id=1, source_target_pairs={{0,1},{1,0},{2,3},{3,2},{4,5},{5,4},{6,7},{7,6},{8,9},{9,8},{10,11... | collective-permute-start | bytes 2162696 | tf_op jit(solution)/shard_map/ppermute | solution.py:229
  8.9 2.2 %collective-permute-done = f32[16,88,128]{2,1,0:T(8,128)S(1)} collective-permute-done((f32[16,88,128]{2,1,0:T(8,128)S(1)}, f32[16,88,128]{2,1,0:T(8,128)S(1)}, u32[]{:S(2)}, u32[]{:S(2)}) %collective-permute-start) | collective-permute-done | bytes 720928 | tf_op jit(solution)/shard_map/ppermute | solution.py:229
  11.0 0.1 add.3
  11.2 20.8 %all_to_all.15.in_ref = f32[16,88,128]{2,1,0:T(8,128)S(1)} all-to-all(f32[16,88,128]{2,1,0:T(8,128)S(1)} %add.3), channel_id=1, replica_groups=mesh['y'=4,'z'=16,'x'=4,'c'=2] {'y','x'}, dimensions={0} | all-to-all | bytes 1441792 | tf_op jit(solution)/shard_map/all_to_all | solution.py:223
  31.9 0.1 plane_sum.1
  32.0 32.5 %all_to_all.16.in_ref = f32[16,32,128]{2,1,0:T(8,128)S(1)} all-to-all(f32[16,32,128]{2,1,0:T(8,128)S(1)} %bitcast.3), channel_id=1, replica_groups=mesh['y'=4,'z'=16,'x'=4,'c'=2] {'z'}, dimensions={0} | all-to-all | bytes 524288 | tf_op jit(solution)/shard_map/all_to_all | solution.py:223
  64.6 11.5 %all_to_all.17 = f32[16,24,128]{2,1,0:T(8,128)S(1)} all-to-all(f32[16,24,128]{2,1,0:T(8,128)S(1)} %get-tuple-element.8), channel_id=1, replica_groups=mesh['y'=4,'z'=16,'x'=4,'c'=2] {'y','x'}, dimensions={0} | all-to-all | bytes 393216 | tf_op jit(solution)/shard_map/all_to_all | solution.py:223
  76.1 8.3 %factor.1 = (f32[256,256]{1,0:T(8,128)}, f32[2,256]{1,0:T(2,128)}) custom-call(f32[384,128]{1,0:T(8,128)S(1)} %bitcast.4, f32[8,128]{1,0:T(8,128)S(1)} %get-tuple-element.9.c_ref), custom_call_target="tpu_custom_call" | custom-call | tf_op jit(solution)/shard_map/factor/pallas_call | solution.py:101
  (1 shorter events, 0.0 us)
Async XLA Ops:
  7.0 4.1 %collective-permute-start = (f32[16,88,128]{2,1,0:T(8,128)S(1)}, f32[16,88,128]{2,1,0:T(8,128)S(1)}, u32[]{:S(2)}, u32[]{:S(2)}) collective-permute-start(f32[16,88,128]{2,1,0:T(8,128)S(1)} %get-tuple-element.7), channel_id=1, source_target_pairs={{0,1},{1,0},{2,3},{3,2},{4,5},{5,4},{6,7},{7,6},{8,9},{9,8},{10,11... | collective-permute-start | bytes 2162696 | tf_op jit(solution)/shard_map/ppermute | solution.py:229

commit v4 on v3

--- a/solution.py
+++ b/solution.py
@@ -67,17 +67,25 @@
 def blocks(x): return [x[8*i:8*i+8, :] for i in range(x.shape[0]//8)]
 def cat(bs): return jnp.concatenate(bs, axis=0)
 
-def chol_kernel(scale, g_ref, c_ref, r_ref, p_ref):
+def chol_kernel(scale, core_ref, own_ref, other_ref, c_ref, r_ref, p_ref):
     lane = lax.broadcasted_iota(jnp.int32, (128, 128), 1)
     sub = lax.broadcasted_iota(jnp.int32, (128, 128), 0)
     eye = lane == sub
-    a11, a21, a22 = g_ref[0:128, :], g_ref[128:256, :], g_ref[256:384, :]
+    first = core_ref[0] == 0
+    upper = sub[0:8] < 4
+    tiles, tails = [], []
+    for n in range(16):
+        own, other = own_ref[n], other_ref[n]
+        one, two = jnp.where(first, own, other), jnp.where(first, other, own)
+        tiles += [one[0:8], two[0:8]]
+        tails.append(jnp.where(upper, one[8:16], pltpu.roll(two[8:16], 4, 0)))
+    a11, a21, a22 = cat(tiles[0:16]), cat(tiles[16:32]), cat(tails)
     def diag(x):
         e = jnp.where(eye, x, 0.0)
         return jnp.sum(e, axis=0, keepdims=True), jnp.sum(e, axis=1, keepdims=True)
     l1, s1 = diag(a11); l2, s2 = diag(a22)
     il1, is1, il2, is2 = map(lax.rsqrt, (l1, s1, l2, s2))
-    c1, c2 = c_ref[0:8, :] * il1, pltpu.roll(c_ref[...], 6, 0) * il2
+    c1, c2 = pltpu.roll(c_ref[...], 4, 0) * il1, pltpu.roll(c_ref[...], 2, 0) * il2
     a11 = a11 * is1 * il1
     a21 = a21 * is2 * il1
     a22 = a22 * is2 * il2
@@ -97,11 +105,17 @@
     p_ref[:, 0:128] = p1[0:2]
     p_ref[:, 128:256] = p2[0:2]
 
-def chol(g, c, scale, **kw):
-    return pl.pallas_call(functools.partial(chol_kernel, scale),
-        out_shape=(jax.ShapeDtypeStruct((256,256),jnp.float32), jax.ShapeDtypeStruct((2,256),jnp.float32)), **kw)(g, c)
-
-GRAM_ROWS = 24
+def chol(core, own, other, c, scale):
+    vmem = pl.BlockSpec(memory_space=pltpu.VMEM)
+    return pl.pallas_call(
+        functools.partial(chol_kernel, scale),
+        in_specs=[pl.BlockSpec(memory_space=pltpu.SMEM), vmem, vmem, vmem],
+        out_shape=(jax.ShapeDtypeStruct((256, 256), jnp.float32), jax.ShapeDtypeStruct((2, 256), jnp.float32)),
+        compiler_params=SMALL,
+        name="factor",
+    )(core, own, other, c)
+
+GRAM_ROWS = 16
 CROSS_ROWS = 64
 PLANE = 16
 RING = 16
@@ -132,11 +146,16 @@
     mixed = gram[256:512]
     whole = gram[0:256] + mixed + mixed.T
     packed = jnp.concatenate([whole[0:128, 0:128], whole[128:256, 0:128], whole[128:256, 128:256]], axis=0)
+    core = core_ref[0]
+    upper = lax.broadcasted_iota(jnp.int32, (8, 128), 0) < 4
     for peer in range(PLANE):
-        part = packed[peer * GRAM_ROWS : (peer + 1) * GRAM_ROWS]
-        keep_ref[peer, 0:GRAM_ROWS, :] = part
-        send_ref[peer, 0:GRAM_ROWS, :] = part
-    core = core_ref[0]
+        one, two = packed[peer * 16 : peer * 16 + 8], packed[peer * 16 + 8 : peer * 16 + 16]
+        tail = packed[256 + peer * 8 : 264 + peer * 8]
+        turned = pltpu.roll(tail, 4, 0)
+        keep_ref[peer, 0:8, :] = jnp.where(core == 0, one, two)
+        send_ref[peer, 0:8, :] = jnp.where(core == 0, two, one)
+        keep_ref[peer, 8:16, :] = jnp.where(upper, jnp.where(core == 0, tail, turned), 0.0)
+        send_ref[peer, 8:16, :] = jnp.where(upper, jnp.where(core == 0, turned, tail), 0.0)
     for y in range(4):
         cols = slice(y * 256, y * 256 + 256)
         cross = jnp.dot(pair[...], deform[:, cols], preferred_element_type=jnp.float32)
@@ -179,23 +198,21 @@
     total = in_ref[0]
     for peer in range(1, PLANE):
         total = total + in_ref[peer]
-    spare = jnp.zeros((4, 128), jnp.float32)
     for z in range(RING):
-        out_ref[z * 32 : z * 32 + GRAM_ROWS, :] = total[0:GRAM_ROWS]
-        out_ref[z * 32 + 28 : z * 32 + 32, :] = spare
+        out_ref[z * 16 : z * 16 + 16, :] = total[0:GRAM_ROWS]
     for q in range(4):
         at = GRAM_ROWS + q * RING
-        out_ref[pl.ds(GRAM_ROWS + q, RING, stride=32), :] = total[at : at + RING]
+        out_ref[pl.ds(12 + q, RING, stride=16), :] = total[at : at + RING]
 
 
 def plane_sum(arrived):
     out = pl.pallas_call(
         plane_kernel,
-        out_shape=jax.ShapeDtypeStruct((RING * 32, 128), jnp.float32),
+        out_shape=jax.ShapeDtypeStruct((RING * 16, 128), jnp.float32),
         compiler_params=SMALL,
         name="plane_sum",
     )(arrived)
-    return out.reshape(RING, 32, 128)
+    return out.reshape(RING, 16, 128)
 
 
 def ring_kernel(in_ref, chunk_ref, own_ref):
@@ -203,8 +220,8 @@
     for z in range(1, RING):
         total = total + in_ref[z]
     for peer in range(PLANE):
-        chunk_ref[peer] = total[0:GRAM_ROWS]
-    own_ref[...] = total[GRAM_ROWS:32]
+        chunk_ref[peer] = total
+    own_ref[...] = total[8:16]
 
 
 def ring_sum(arrived):
@@ -226,12 +243,13 @@
 def body(deform, sketch):
     core = lax.axis_index("c").astype(jnp.int32).reshape(1)
     keep, send = front(deform, sketch, core)
-    chip = keep + lax.ppermute(send, "c", [(0, 1), (1, 0)])
+    cores = [(0, 1), (1, 0)]
+    chip = keep + lax.ppermute(send, "c", cores)
     own_plane = plane_sum(swap(chip, ("y", "x")))
     chunks, own = ring_sum(swap(own_plane, ("z",)))
-    packed = swap(chunks, ("y", "x")).reshape(384, 128)
+    mine = swap(chunks, ("y", "x"))
     total_rows = deform.shape[0] * lax.axis_size(("y", "z", "x", "c"))
-    return chol(packed, own, 1.0 / float(np.sqrt(np.float32(total_rows))), compiler_params=SMALL, name="factor")
+    return chol(core, mine, lax.ppermute(mine, "c", cores), own, 1.0 / float(np.sqrt(np.float32(total_rows))))
 
 
 def solution(mesh):

time: 84.7 us -> 84.6 us (level)
  the two profiles are of different devices: /device:TPU:32 before, /device:TPU:1 now
where the time goes in v4:
time: 84.6 us; the launch traced here: 84.3 us
  blocking collectives  50.3 us (59%)
  starting transfers between devices  15.8 us (19%)
  Pallas kernels  14.7 us (17%)
  waiting for transfers between devices  2.67 us (3%)
    all_to_all x3, blocking collectives, swap(): return lax.all_to_all(values, axis, split_axis=0, concat_axis=0, tiled=True)  50.3 us
    ppermute x1, starting transfers between devices, body(): chip = keep + lax.ppermute(send, 'c', cores)  8.75 us
    pallas_call x1, Pallas kernels, chol(): pl.pallas_call(functools.partial(chol_kernel, scale), in_specs=[pl.BlockS...  8.33 us
    ppermute x1, starting transfers between devices, body(): lax.ppermute(mine, 'c', cores)  7.09 us
    pallas_call x1, Pallas kernels, front(): pl.pallas_call(front_kernel, in_specs=[pl.BlockSpec(memory_space=pltpu.SM...  6.32 us
    ppermute x1, waiting for transfers between devices, body(): chip = keep + lax.ppermute(send, 'c', cores)  1.7 us
  transfers between devices with their start and end apart: 2, of which 2 were waited for; matrix products, arithmetic and copies ran while one was open for 0% of the time, Pallas kernels for 0%

profile of v4, /device:TPU:1, one launch (start us, length us, event | category | flops | bytes accessed | tf_op | source)
XLA Modules:
  0.0 84.3 jit_solution(10287956607903669504)
XLA Ops:
  0.6 6.3 %front.1 = (f32[16,80,128]{2,1,0:T(8,128)S(1)}, f32[16,80,128]{2,1,0:T(8,128)S(1)}) custom-call(s32[1]{0:T(128)} %bitcast.core_ref, bf16[2048,1024]{1,0:T(8,128)(2,1)} %deform_hbm.1, bf16[1024,256]{1,0:T(8,128)(2,1)} %sketch_hbm.1), custom_call_target="tpu_custom_call" | custom-call | tf_op jit(solution)/shard_map/front/pallas_call | solution.py:179
  7.0 8.7 %collective-permute-start = (f32[16,80,128]{2,1,0:T(8,128)S(1)}, f32[16,80,128]{2,1,0:T(8,128)S(1)}, u32[]{:S(2)}, u32[]{:S(2)}) collective-permute-start(f32[16,80,128]{2,1,0:T(8,128)S(1)} %get-tuple-element.7), channel_id=1, source_target_pairs={{0,1},{1,0},{2,3},{3,2},{4,5},{5,4},{6,7},{7,6},{8,9},{9,8},{10,11... | collective-permute-start | bytes 1966088 | tf_op jit(solution)/shard_map/ppermute | solution.py:247
  15.7 1.7 %collective-permute-done = f32[16,80,128]{2,1,0:T(8,128)S(1)} collective-permute-done((f32[16,80,128]{2,1,0:T(8,128)S(1)}, f32[16,80,128]{2,1,0:T(8,128)S(1)}, u32[]{:S(2)}, u32[]{:S(2)}) %collective-permute-start) | collective-permute-done | bytes 655392 | tf_op jit(solution)/shard_map/ppermute | solution.py:247
  17.4 0.1 add.3
  17.5 15.3 %all_to_all.15.in_ref = f32[16,80,128]{2,1,0:T(8,128)S(1)} all-to-all(f32[16,80,128]{2,1,0:T(8,128)S(1)} %add.3), channel_id=1, replica_groups=mesh['y'=4,'z'=16,'x'=4,'c'=2] {'y','x'}, dimensions={0} | all-to-all | bytes 1310720 | tf_op jit(solution)/shard_map/all_to_all | solution.py:240
  32.8 25.1 %all_to_all.16.in_ref = f32[16,16,128]{2,1,0:T(8,128)S(1)} all-to-all(f32[16,16,128]{2,1,0:T(8,128)S(1)} %bitcast.2), channel_id=1, replica_groups=mesh['y'=4,'z'=16,'x'=4,'c'=2] {'z'}, dimensions={0} | all-to-all | bytes 262144 | tf_op jit(solution)/shard_map/all_to_all | solution.py:240
  57.9 10.0 %all_to_all.17.own_ref = f32[16,16,128]{2,1,0:T(8,128)S(1)} all-to-all(f32[16,16,128]{2,1,0:T(8,128)S(1)} %get-tuple-element.8), channel_id=1, replica_groups=mesh['y'=4,'z'=16,'x'=4,'c'=2] {'y','x'}, dimensions={0} | all-to-all | bytes 262144 | tf_op jit(solution)/shard_map/all_to_all | solution.py:240
  67.9 7.1 %collective-permute-start.1 = (f32[16,16,128]{2,1,0:T(8,128)S(1)}, f32[16,16,128]{2,1,0:T(8,128)S(1)}, u32[]{:S(2)}, u32[]{:S(2)}) collective-permute-start(f32[16,16,128]{2,1,0:T(8,128)S(1)} %all_to_all.17.own_ref), channel_id=1, source_target_pairs={{0,1},{1,0},{2,3},{3,2},{4,5},{5,4},{6,7},{7,6},{8,9},{9,8},{10,11... | collective-permute-start | bytes 393224 | tf_op jit(solution)/shard_map/ppermute | solution.py:252
  75.0 1.0 %collective-permute-done.1.other_ref = f32[16,16,128]{2,1,0:T(8,128)S(1)} collective-permute-done((f32[16,16,128]{2,1,0:T(8,128)S(1)}, f32[16,16,128]{2,1,0:T(8,128)S(1)}, u32[]{:S(2)}, u32[]{:S(2)}) %collective-permute-start.1) | collective-permute-done | bytes 131104 | tf_op jit(solution)/shard_map/ppermute | solution.py:252
  76.0 8.3 %factor.1 = (f32[256,256]{1,0:T(8,128)}, f32[2,256]{1,0:T(2,128)}) custom-call(s32[1]{0:T(128)} %bitcast.core_ref, f32[16,16,128]{2,1,0:T(8,128)S(1)} %all_to_all.17.own_ref, f32[16,16,128]{2,1,0:T(8,128)S(1)} %collective-permute-done.1.other_ref, f32[8,128]{1,0:T(8,128)S(1)} %get-tuple-element.9.c_ref), custom_call_target="tpu_custom_call" | custom-call | tf_op jit(solution)/shard_map/factor/pallas_call | solution.py:110
  (2 shorter events, 0.1 us)
Async XLA Ops:
  7.0 10.5 %collective-permute-start = (f32[16,80,128]{2,1,0:T(8,128)S(1)}, f32[16,80,128]{2,1,0:T(8,128)S(1)}, u32[]{:S(2)}, u32[]{:S(2)}) collective-permute-start(f32[16,80,128]{2,1,0:T(8,128)S(1)} %get-tuple-element.7), channel_id=1, source_target_pairs={{0,1},{1,0},{2,3},{3,2},{4,5},{5,4},{6,7},{7,6},{8,9},{9,8},{10,11... | collective-permute-start | bytes 1966088 | tf_op jit(solution)/shard_map/ppermute | solution.py:247
  67.9 8.1 %collective-permute-start.1 = (f32[16,16,128]{2,1,0:T(8,128)S(1)}, f32[16,16,128]{2,1,0:T(8,128)S(1)}, u32[]{:S(2)}, u32[]{:S(2)}) collective-permute-start(f32[16,16,128]{2,1,0:T(8,128)S(1)} %all_to_all.17.own_ref), channel_id=1, source_target_pairs={{0,1},{1,0},{2,3},{3,2},{4,5},{5,4},{6,7},{7,6},{8,9},{9,8},{10,11... | collective-permute-start | bytes 393224 | tf_op jit(solution)/shard_map/ppermute | solution.py:252

commit v5 on v4

--- a/solution.py
+++ b/solution.py
@@ -67,19 +67,23 @@
 def blocks(x): return [x[8*i:8*i+8, :] for i in range(x.shape[0]//8)]
 def cat(bs): return jnp.concatenate(bs, axis=0)
 
-def chol_kernel(scale, core_ref, own_ref, other_ref, c_ref, r_ref, p_ref):
+def chol_kernel(scale, g_ref, c_ref, r_ref, p_ref):
     lane = lax.broadcasted_iota(jnp.int32, (128, 128), 1)
     sub = lax.broadcasted_iota(jnp.int32, (128, 128), 0)
     eye = lane == sub
-    first = core_ref[0] == 0
     upper = sub[0:8] < 4
-    tiles, tails = [], []
+    tiles = []
     for n in range(16):
-        own, other = own_ref[n], other_ref[n]
-        one, two = jnp.where(first, own, other), jnp.where(first, other, own)
-        tiles += [one[0:8], two[0:8]]
-        tails.append(jnp.where(upper, one[8:16], pltpu.roll(two[8:16], 4, 0)))
-    a11, a21, a22 = cat(tiles[0:16]), cat(tiles[16:32]), cat(tails)
+        tiles += [g_ref[n, 0:8, :], g_ref[n, 8:16, :]]
+    for n in range(8):
+        tiles.append(jnp.where(upper, g_ref[2*n, 16:24, :], pltpu.roll(g_ref[2*n+1, 16:24, :], 4, 0)))
+    corner = (sub < 64) & (lane >= 64)
+    def mirrored(x):
+        return jnp.where(corner, x.T, x)
+    top = cat(tiles[0:8])
+    a11 = mirrored(cat([top] + tiles[8:16]))
+    a21 = cat(tiles[16:32])
+    a22 = mirrored(cat([pltpu.roll(top, 64, 1)] + tiles[32:40]))
     def diag(x):
         e = jnp.where(eye, x, 0.0)
         return jnp.sum(e, axis=0, keepdims=True), jnp.sum(e, axis=1, keepdims=True)
@@ -105,17 +109,15 @@
     p_ref[:, 0:128] = p1[0:2]
     p_ref[:, 128:256] = p2[0:2]
 
-def chol(core, own, other, c, scale):
-    vmem = pl.BlockSpec(memory_space=pltpu.VMEM)
+def chol(g, c, scale):
     return pl.pallas_call(
         functools.partial(chol_kernel, scale),
-        in_specs=[pl.BlockSpec(memory_space=pltpu.SMEM), vmem, vmem, vmem],
         out_shape=(jax.ShapeDtypeStruct((256, 256), jnp.float32), jax.ShapeDtypeStruct((2, 256), jnp.float32)),
         compiler_params=SMALL,
         name="factor",
-    )(core, own, other, c)
-
-GRAM_ROWS = 16
+    )(g, c)
+
+GRAM_ROWS = 24
 CROSS_ROWS = 64
 PLANE = 16
 RING = 16
@@ -145,17 +147,19 @@
     gram = lax.dot_general(pair[...], pair[0:256, :], NT, preferred_element_type=jnp.float32)
     mixed = gram[256:512]
     whole = gram[0:256] + mixed + mixed.T
-    packed = jnp.concatenate([whole[0:128, 0:128], whole[128:256, 0:128], whole[128:256, 128:256]], axis=0)
     core = core_ref[0]
-    upper = lax.broadcasted_iota(jnp.int32, (8, 128), 0) < 4
+    sub = lax.broadcasted_iota(jnp.int32, (8, 128), 0)
+    low = lax.broadcasted_iota(jnp.int32, (64, 128), 1) < 64
+    corners = jnp.where(low, whole[0:64, 0:128], pltpu.roll(whole[128:192, 128:256], 64, 1))
+    packed = jnp.concatenate([corners, whole[64:128, 0:128], whole[128:256, 0:128], whole[192:256, 128:256]], axis=0)
     for peer in range(PLANE):
-        one, two = packed[peer * 16 : peer * 16 + 8], packed[peer * 16 + 8 : peer * 16 + 16]
-        tail = packed[256 + peer * 8 : 264 + peer * 8]
-        turned = pltpu.roll(tail, 4, 0)
-        keep_ref[peer, 0:8, :] = jnp.where(core == 0, one, two)
-        send_ref[peer, 0:8, :] = jnp.where(core == 0, two, one)
-        keep_ref[peer, 8:16, :] = jnp.where(upper, jnp.where(core == 0, tail, turned), 0.0)
-        send_ref[peer, 8:16, :] = jnp.where(upper, jnp.where(core == 0, turned, tail), 0.0)
+        tile = 256 + peer // 2 * 8
+        tail = packed[tile : tile + 8]
+        if peer % 2:
+            tail = pltpu.roll(tail, 4, 0)
+        for ref in (keep_ref, send_ref):
+            ref[peer, 0:16, :] = packed[peer * 16 : peer * 16 + 16]
+            ref[peer, 16:24, :] = jnp.where(sub < 4, tail, 0.0)
     for y in range(4):
         cols = slice(y * 256, y * 256 + 256)
         cross = jnp.dot(pair[...], deform[:, cols], preferred_element_type=jnp.float32)
@@ -199,20 +203,20 @@
     for peer in range(1, PLANE):
         total = total + in_ref[peer]
     for z in range(RING):
-        out_ref[z * 16 : z * 16 + 16, :] = total[0:GRAM_ROWS]
+        out_ref[z * 24 : z * 24 + 24, :] = total[0:GRAM_ROWS]
     for q in range(4):
         at = GRAM_ROWS + q * RING
-        out_ref[pl.ds(12 + q, RING, stride=16), :] = total[at : at + RING]
+        out_ref[pl.ds(20 + q, RING, stride=24), :] = total[at : at + RING]
 
 
 def plane_sum(arrived):
     out = pl.pallas_call(
         plane_kernel,
-        out_shape=jax.ShapeDtypeStruct((RING * 16, 128), jnp.float32),
+        out_shape=jax.ShapeDtypeStruct((RING * 24, 128), jnp.float32),
         compiler_params=SMALL,
         name="plane_sum",
     )(arrived)
-    return out.reshape(RING, 16, 128)
+    return out.reshape(RING, 24, 128)
 
 
 def ring_kernel(in_ref, chunk_ref, own_ref):
@@ -221,7 +225,7 @@
         total = total + in_ref[z]
     for peer in range(PLANE):
         chunk_ref[peer] = total
-    own_ref[...] = total[8:16]
+    own_ref[...] = total[16:24]
 
 
 def ring_sum(arrived):
@@ -249,7 +253,7 @@
     chunks, own = ring_sum(swap(own_plane, ("z",)))
     mine = swap(chunks, ("y", "x"))
     total_rows = deform.shape[0] * lax.axis_size(("y", "z", "x", "c"))
-    return chol(core, mine, lax.ppermute(mine, "c", cores), own, 1.0 / float(np.sqrt(np.float32(total_rows))))
+    return chol(mine, own, 1.0 / float(np.sqrt(np.float32(total_rows))))
 
 
 def solution(mesh):

time: 84.6 us -> 82.9 us (0.980)
  the two profiles are of different devices: /device:TPU:1 before, /device:TPU:32 now
where the time goes in v5:
time: 82.9 us; the launch traced here: 82.7 us
  blocking collectives  63 us (76%)
  Pallas kernels  14.9 us (18%)
  waiting for transfers between devices  2.16 us (3%)
  starting transfers between devices  1.92 us (2%)
    all_to_all x3, blocking collectives, swap(): return lax.all_to_all(values, axis, split_axis=0, concat_axis=0, tiled=True)  63 us
    pallas_call x1, Pallas kernels, chol(): pl.pallas_call(functools.partial(chol_kernel, scale), out_shape=(jax.Shap...  8.5 us
    pallas_call x1, Pallas kernels, front(): pl.pallas_call(front_kernel, in_specs=[pl.BlockSpec(memory_space=pltpu.SM...  6.32 us
    ppermute x1, waiting for transfers between devices, body(): chip = keep + lax.ppermute(send, 'c', cores)  2.16 us
    ppermute x1, starting transfers between devices, body(): chip = keep + lax.ppermute(send, 'c', cores)  1.92 us
  transfers between devices with their start and end apart: 1, of which 1 were waited for; matrix products, arithmetic and copies ran while one was open for 0% of the time, Pallas kernels for 0%

profile of v5, /device:TPU:32, one launch (start us, length us, event | category | flops | bytes accessed | tf_op | source)
XLA Modules:
  0.0 82.7 jit_solution(8508462057278206787)
XLA Ops:
  0.6 6.3 %front.1 = (f32[16,88,128]{2,1,0:T(8,128)S(1)}, f32[16,88,128]{2,1,0:T(8,128)S(1)}) custom-call(s32[1]{0:T(128)} %bitcast.core_ref, bf16[2048,1024]{1,0:T(8,128)(2,1)} %deform_hbm.1, bf16[1024,256]{1,0:T(8,128)(2,1)} %sketch_hbm.1), custom_call_target="tpu_custom_call" | custom-call | tf_op jit(solution)/shard_map/front/pallas_call | solution.py:183
  7.0 1.9 %collective-permute-start = (f32[16,88,128]{2,1,0:T(8,128)S(1)}, f32[16,88,128]{2,1,0:T(8,128)S(1)}, u32[]{:S(2)}, u32[]{:S(2)}) collective-permute-start(f32[16,88,128]{2,1,0:T(8,128)S(1)} %get-tuple-element.7), channel_id=1, source_target_pairs={{0,1},{1,0},{2,3},{3,2},{4,5},{5,4},{6,7},{7,6},{8,9},{9,8},{10,11... | collective-permute-start | bytes 2162696 | tf_op jit(solution)/shard_map/ppermute | solution.py:251
  8.9 2.2 %collective-permute-done = f32[16,88,128]{2,1,0:T(8,128)S(1)} collective-permute-done((f32[16,88,128]{2,1,0:T(8,128)S(1)}, f32[16,88,128]{2,1,0:T(8,128)S(1)}, u32[]{:S(2)}, u32[]{:S(2)}) %collective-permute-start) | collective-permute-done | bytes 720928 | tf_op jit(solution)/shard_map/ppermute | solution.py:251
  11.0 0.1 add.3
  11.2 20.8 %all_to_all.15.in_ref = f32[16,88,128]{2,1,0:T(8,128)S(1)} all-to-all(f32[16,88,128]{2,1,0:T(8,128)S(1)} %add.3), channel_id=1, replica_groups=mesh['y'=4,'z'=16,'x'=4,'c'=2] {'y','x'}, dimensions={0} | all-to-all | bytes 1441792 | tf_op jit(solution)/shard_map/all_to_all | solution.py:244
  32.0 30.8 %all_to_all.16.in_ref = f32[16,24,128]{2,1,0:T(8,128)S(1)} all-to-all(f32[16,24,128]{2,1,0:T(8,128)S(1)} %bitcast.2), channel_id=1, replica_groups=mesh['y'=4,'z'=16,'x'=4,'c'=2] {'z'}, dimensions={0} | all-to-all | bytes 393216 | tf_op jit(solution)/shard_map/all_to_all | solution.py:244
  62.8 11.3 %all_to_all.17.g_ref = f32[16,24,128]{2,1,0:T(8,128)S(1)} all-to-all(f32[16,24,128]{2,1,0:T(8,128)S(1)} %get-tuple-element.8), channel_id=1, replica_groups=mesh['y'=4,'z'=16,'x'=4,'c'=2] {'y','x'}, dimensions={0} | all-to-all | bytes 393216 | tf_op jit(solution)/shard_map/all_to_all | solution.py:244
  74.2 8.5 %factor.1 = (f32[256,256]{1,0:T(8,128)}, f32[2,256]{1,0:T(2,128)}) custom-call(f32[16,24,128]{2,1,0:T(8,128)S(1)} %all_to_all.17.g_ref, f32[8,128]{1,0:T(8,128)S(1)} %get-tuple-element.9.c_ref), custom_call_target="tpu_custom_call" | custom-call | tf_op jit(solution)/shard_map/factor/pallas_call | solution.py:113
  (2 shorter events, 0.1 us)
Async XLA Ops:
  7.0 4.1 %collective-permute-start = (f32[16,88,128]{2,1,0:T(8,128)S(1)}, f32[16,88,128]{2,1,0:T(8,128)S(1)}, u32[]{:S(2)}, u32[]{:S(2)}) collective-permute-start(f32[16,88,128]{2,1,0:T(8,128)S(1)} %get-tuple-element.7), channel_id=1, source_target_pairs={{0,1},{1,0},{2,3},{3,2},{4,5},{5,4},{6,7},{7,6},{8,9},{9,8},{10,11... | collective-permute-start | bytes 2162696 | tf_op jit(solution)/shard_map/ppermute | solution.py:251

commit v6 on v5

--- a/solution.py
+++ b/solution.py
@@ -174,8 +174,8 @@
                 for i in range(2):
                     at = GRAM_ROWS + (half * 2 + i) * RING
                     base = y * 256 + x * 4 + i
-                    keep_ref[y * 4 + x, at : at + RING, :] = lines[half, pl.ds(base + core * 2, RING, stride=16), :]
-                    send_ref[y * 4 + x, at : at + RING, :] = lines[half, pl.ds(base + 2 - core * 2, RING, stride=16), :]
+                    keep_ref[x * 4 + y, at : at + RING, :] = lines[half, pl.ds(base + core * 2, RING, stride=16), :]
+                    send_ref[x * 4 + y, at : at + RING, :] = lines[half, pl.ds(base + 2 - core * 2, RING, stride=16), :]
 
 
 def front(deform, sketch, core):
@@ -249,9 +249,9 @@
     keep, send = front(deform, sketch, core)
     cores = [(0, 1), (1, 0)]
     chip = keep + lax.ppermute(send, "c", cores)
-    own_plane = plane_sum(swap(chip, ("y", "x")))
+    own_plane = plane_sum(swap(chip, ("x", "y")))
     chunks, own = ring_sum(swap(own_plane, ("z",)))
-    mine = swap(chunks, ("y", "x"))
+    mine = swap(chunks, ("x", "y"))
     total_rows = deform.shape[0] * lax.axis_size(("y", "z", "x", "c"))
     return chol(mine, own, 1.0 / float(np.sqrt(np.float32(total_rows))))
 

time: 82.9 us -> 82.8 us (level)
  no operation moved by 1% of the time
where the time goes in v6:
time: 82.8 us; the launch traced here: 82.6 us
  blocking collectives  62.8 us (76%)
  Pallas kernels  14.9 us (18%)
  waiting for transfers between devices  2.16 us (3%)
  starting transfers between devices  1.92 us (2%)
    all_to_all x3, blocking collectives, swap(): return lax.all_to_all(values, axis, split_axis=0, concat_axis=0, tiled=True)  62.8 us
    pallas_call x1, Pallas kernels, chol(): pl.pallas_call(functools.partial(chol_kernel, scale), out_shape=(jax.Shap...  8.5 us
    pallas_call x1, Pallas kernels, front(): pl.pallas_call(front_kernel, in_specs=[pl.BlockSpec(memory_space=pltpu.SM...  6.32 us
    ppermute x1, waiting for transfers between devices, body(): chip = keep + lax.ppermute(send, 'c', cores)  2.16 us
    ppermute x1, starting transfers between devices, body(): chip = keep + lax.ppermute(send, 'c', cores)  1.92 us
  transfers between devices with their start and end apart: 1, of which 1 were waited for; matrix products, arithmetic and copies ran while one was open for 0% of the time, Pallas kernels for 0%

profile of v6, /device:TPU:32, one launch (start us, length us, event | category | flops | bytes accessed | tf_op | source)
XLA Modules:
  0.0 82.6 jit_solution(3713894059899695370)
XLA Ops:
  0.6 6.3 %front.1 = (f32[16,88,128]{2,1,0:T(8,128)S(1)}, f32[16,88,128]{2,1,0:T(8,128)S(1)}) custom-call(s32[1]{0:T(128)} %bitcast.core_ref, bf16[2048,1024]{1,0:T(8,128)(2,1)} %deform_hbm.1, bf16[1024,256]{1,0:T(8,128)(2,1)} %sketch_hbm.1), custom_call_target="tpu_custom_call" | custom-call | tf_op jit(solution)/shard_map/front/pallas_call | solution.py:183
  7.0 1.9 %collective-permute-start = (f32[16,88,128]{2,1,0:T(8,128)S(1)}, f32[16,88,128]{2,1,0:T(8,128)S(1)}, u32[]{:S(2)}, u32[]{:S(2)}) collective-permute-start(f32[16,88,128]{2,1,0:T(8,128)S(1)} %get-tuple-element.7), channel_id=1, source_target_pairs={{0,1},{1,0},{2,3},{3,2},{4,5},{5,4},{6,7},{7,6},{8,9},{9,8},{10,11... | collective-permute-start | bytes 2162696 | tf_op jit(solution)/shard_map/ppermute | solution.py:251
  8.9 2.2 %collective-permute-done = f32[16,88,128]{2,1,0:T(8,128)S(1)} collective-permute-done((f32[16,88,128]{2,1,0:T(8,128)S(1)}, f32[16,88,128]{2,1,0:T(8,128)S(1)}, u32[]{:S(2)}, u32[]{:S(2)}) %collective-permute-start) | collective-permute-done | bytes 720928 | tf_op jit(solution)/shard_map/ppermute | solution.py:251
  11.0 0.1 add.3
  11.2 20.6 %all_to_all.15.in_ref = f32[16,88,128]{2,1,0:T(8,128)S(1)} all-to-all(f32[16,88,128]{2,1,0:T(8,128)S(1)} %add.3), channel_id=1, replica_groups=mesh['y'=4,'z'=16,'x'=4,'c'=2] {'x','y'}, dimensions={0} | all-to-all | bytes 1441792 | tf_op jit(solution)/shard_map/all_to_all | solution.py:244
  31.8 30.4 %all_to_all.16.in_ref = f32[16,24,128]{2,1,0:T(8,128)S(1)} all-to-all(f32[16,24,128]{2,1,0:T(8,128)S(1)} %bitcast.2), channel_id=1, replica_groups=mesh['y'=4,'z'=16,'x'=4,'c'=2] {'z'}, dimensions={0} | all-to-all | bytes 393216 | tf_op jit(solution)/shard_map/all_to_all | solution.py:244
  62.2 11.8 %all_to_all.17.g_ref = f32[16,24,128]{2,1,0:T(8,128)S(1)} all-to-all(f32[16,24,128]{2,1,0:T(8,128)S(1)} %get-tuple-element.8), channel_id=1, replica_groups=mesh['y'=4,'z'=16,'x'=4,'c'=2] {'x','y'}, dimensions={0} | all-to-all | bytes 393216 | tf_op jit(solution)/shard_map/all_to_all | solution.py:244
  74.1 8.5 %factor.1 = (f32[256,256]{1,0:T(8,128)}, f32[2,256]{1,0:T(2,128)}) custom-call(f32[16,24,128]{2,1,0:T(8,128)S(1)} %all_to_all.17.g_ref, f32[8,128]{1,0:T(8,128)S(1)} %get-tuple-element.9.c_ref), custom_call_target="tpu_custom_call" | custom-call | tf_op jit(solution)/shard_map/factor/pallas_call | solution.py:113
  (2 shorter events, 0.1 us)
Async XLA Ops:
  7.0 4.1 %collective-permute-start = (f32[16,88,128]{2,1,0:T(8,128)S(1)}, f32[16,88,128]{2,1,0:T(8,128)S(1)}, u32[]{:S(2)}, u32[]{:S(2)}) collective-permute-start(f32[16,88,128]{2,1,0:T(8,128)S(1)} %get-tuple-element.7), channel_id=1, source_target_pairs={{0,1},{1,0},{2,3},{3,2},{4,5},{5,4},{6,7},{7,6},{8,9},{9,8},{10,11... | collective-permute-start | bytes 2162696 | tf_op jit(solution)/shard_map/ppermute | solution.py:251
